TPU v7x, 32 devices: a whole 2x2x4 slice. The times are simulated.
32 devices in a mesh: section: 8 (over y, x, core), tensor: 4 (over z).
Axes of the slice: x: 2, y: 2, z: 4, core: 2. Of those that a mesh axis runs over, the one named last changes fastest.
Arguments:
- states: bfloat16 [4096, 8192], P('section', 'tensor'), may hold values from -6 to 6
- lengths: int32 [8, 16], P('section'), may hold values from 1 to 96, 512 in all within a row
- routes: int32 [4096, 1], P('section'), may hold values from 0 to 7; in each aligned block of 512 rows (0 to 511, 512 to 1023, ...) at most 128 rows name the same one
- score_gain: float32 [8, 8192], P('section'), may hold values from 0.25 to 1.75
- score_weight: bfloat16 [8, 8192, 4096], P('section', None, 'tensor'), may hold values from -0.0625 to 0.0625
- score_heads: float32 [8, 4096, 2], P('section', 'tensor'), may hold values from -0.09375 to 0.09375
- actor_gain: float32 [8192], replicated, may hold values from 0.25 to 1.75
- actor_weight: bfloat16 [8192, 4096], P(None, 'tensor'), may hold values from -0.0625 to 0.0625
- actor_heads: float32 [4096], P('tensor'), may hold values from -0.09375 to 0.09375
Outputs:
- packed_scores: float32 [2, 8192], P(None, 'section')
- advantages: float32 [4096], P('section')
- actor_grad: float32 [8192, 4096], P('section', 'tensor')
Inputs may be any that keep to these rules, and one draw needn't show every extreme that they name: `lengths`: each row sums to 512; its largest entry is exactly 96. `routes`: in the rows of one section (aligned blocks of 512 rows) no member is named by more than 128 rows; some member is named by exactly 128 rows of some block.
All inputs are finite; a program needn't handle non-finite values.
Results may differ from a plain program's by a relative error of at most 0.0055.
Values may be sent and summed in bfloat16 or wider, within the bound.
A program may use at most 128 MiB of HBM per device.

v0:
```python
import jax
import jax.numpy as jnp
from jax import lax
from jax.sharding import PartitionSpec as P

epsilon = 1e-05
trace_decay = 0.95
penalty = 0.1


def compose(earlier, later):
    return (earlier[0] * later[0], later[1] + later[0] * earlier[1])


def advantage_rows(values, rewards, lengths):
    ends = jnp.cumsum(lengths, axis=1) - 1
    steps_idx = jnp.arange(values.shape[1], dtype=jnp.int32)
    last = jnp.any(steps_idx[None, :, None] == ends[:, None, :], axis=2)
    following = jnp.concatenate([values[:, 1:], jnp.zeros_like(values[:, :1])], axis=1)
    delta = jnp.where(last, rewards, following) - values
    weight = jnp.where(last, 0.0, trace_decay).astype(values.dtype)
    carried = lax.associative_scan(compose, (weight[:, ::-1], delta[:, ::-1]), axis=1)
    return carried[1][:, ::-1]


def body(
    states,
    lengths,
    routes,
    score_gain,
    score_weight,
    score_heads,
    actor_gain,
    actor_weight,
    actor_heads,
):
    sections = lax.axis_size("section")
    tok_count = states.shape[0]
    feat_shard = states.shape[1]
    capacity = 2 * tok_count // sections
    slot_count = sections * capacity
    target = routes[:, 0]
    onehot = (target[:, None] == jnp.arange(sections, dtype=jnp.int32)[None, :]).astype(jnp.int32)
    before = jnp.cumsum(onehot, axis=0) - onehot
    placed = jnp.sum(before * onehot, axis=1)
    slot_index = target * capacity + placed
    dispatch = (jnp.arange(slot_count, dtype=jnp.int32)[:, None] == slot_index[None, :]).astype(
        jnp.bfloat16
    )
    outbox = jnp.dot(dispatch, states, preferred_element_type=jnp.float32).astype(jnp.bfloat16)
    outbox = outbox.reshape(sections, capacity, feat_shard)
    arrived = lax.all_to_all(outbox, "section", split_axis=0, concat_axis=0, tiled=True).reshape(
        slot_count, feat_shard
    )
    gain_row = score_gain[0]
    member_weight = score_weight[0]
    feat_width = gain_row.shape[0]
    widened = lax.all_gather(arrived, "tensor", axis=1, tiled=True).astype(jnp.float32)
    scaled = (widened * gain_row[None, :]).astype(jnp.bfloat16)
    acc_total = jnp.dot(scaled, member_weight, preferred_element_type=jnp.float32)
    acc_total, squares = (acc_total, jnp.sum(widened * widened, axis=1))
    member_scale = lax.rsqrt(squares / feat_width + epsilon)
    preact = acc_total * member_scale[:, None]
    partial_scores = jnp.dot(jax.nn.silu(preact), score_heads[0], precision=lax.Precision.HIGHEST)
    scores = lax.psum(partial_scores, "tensor")
    packed_scores = jnp.transpose(scores)
    returned = lax.all_to_all(
        scores.reshape(sections, capacity, 2), "section", split_axis=0, concat_axis=0, tiled=True
    )
    returned = returned.reshape(slot_count, 2)
    token_scores = jnp.take(returned, slot_index, axis=0)
    raw_adv = advantage_rows(token_scores[:, 0][None, :], token_scores[:, 1][None, :], lengths)[0]
    adv_total, adv_square = lax.psum((jnp.sum(raw_adv), jnp.sum(raw_adv * raw_adv)), "section")
    total_tokens = tok_count * sections
    center = adv_total / total_tokens
    spread = adv_square / total_tokens - center * center
    advantages = (raw_adv - center) * lax.rsqrt(spread + epsilon)
    features = lax.all_gather(states, "tensor", axis=1, tiled=True)
    widened = features.astype(jnp.float32)
    actor_scale = lax.rsqrt(jnp.mean(widened * widened, axis=1) + epsilon)
    gained = (widened * actor_gain[None, :]).astype(jnp.bfloat16)
    actor_pre = (
        jnp.dot(gained, actor_weight, preferred_element_type=jnp.float32) * actor_scale[:, None]
    )
    shift_part = jnp.dot(jax.nn.silu(actor_pre), actor_heads, precision=lax.Precision.HIGHEST)
    log_shift = lax.psum(shift_part, "tensor")
    ratios = jnp.exp(log_shift)
    logit_slope = penalty * (ratios - 1.0) - ratios * advantages
    sigmoid_pre = jax.nn.sigmoid(actor_pre)
    silu_slope = sigmoid_pre * (1.0 + actor_pre * (1.0 - sigmoid_pre))
    grad_pre = ((logit_slope * actor_scale)[:, None] * actor_heads[None, :] * silu_slope).astype(
        jnp.bfloat16
    )
    blocks = lax.all_to_all(gained, "section", split_axis=1, concat_axis=0, tiled=True)
    every_row = lax.all_gather(grad_pre, "section", axis=0, tiled=True)
    actor_grad = lax.dot_general(
        blocks, every_row, (((0,), (0,)), ((), ())), preferred_element_type=jnp.float32
    )
    return (packed_scores, advantages, actor_grad)


def solution(mesh):
    in_specs = (
        P("section", "tensor"),
        P("section", None),
        P("section", None),
        P("section", None),
        P("section", None, "tensor"),
        P("section", "tensor", None),
        P(),
        P(None, "tensor"),
        P("tensor"),
    )
    out_specs = (P(None, "section"), P("section"), P("section", "tensor"))
    return jax.shard_map(body, mesh=mesh, in_specs=in_specs, out_specs=out_specs, check_vma=False)
```

profile of v0, /device:TPU:0, one launch (start us, length us, event | category | flops | bytes accessed | tf_op | source)
XLA Modules:
  0.0 717.2 jit_solution(90734786162934419)
XLA Ops:
  7.2 4.1 copy.28
  11.4 1.1 reduce-window.14
  12.9 2.4 convolution_convert_fusion
  15.3 54.1 %all_to_all.29 = bf16[8,128,2048]{2,1,0:T(8,128)(2,1)} all-to-all(bf16[8,128,2048]{2,1,0:T(8,128)(2,1)S(1)} %bitcast.52), channel_id=1, replica_groups=mesh['section'=8,'tensor'=4] {'section'}, dimensions={0} | all-to-all | bytes 8388608 | tf_op jit(solution)/shard_map/all_to_all | solution.py:52
  69.5 0.6 copy-done.8
  70.4 93.4 %all-gather.6.cloned.1.call-done = bf16[512,8192]{0,1:T(8,128)(2,1)} async-done(((bf16[512,2048]{0,1:T(8,128)(2,1)}), bf16[512,8192]{0,1:T(8,128)(2,1)}) %all-gather.6.cloned.1.call-update) | async-done | bytes 8388624 | tf_op jit(solution)/shard_map/all_gather | solution.py:78
  163.8 5.2 fusion.3
  169.1 15.5 %fusion.43 = f32[512,1024]{1,0:T(8,128)S(1)} fusion(bf16[512,8192]{0,1:T(8,128)(2,1)S(1)} %get-tuple-element.14, bf16[8192,1024]{1,0:T(8,128)(2,1)} %param.16), kind=kOutput, calls=%fused_computation.95 | convolution fusion | flops 8589934592 | bytes 27262976 | tf_op jit(solution)/shard_map/dot_general | solution.py:83
  184.6 2.4 fusion.15
  187.0 263.4 %all-gather.4.cloned.1.call-done = bf16[1024,8192]{1,0:T(8,128)(2,1)} async-done(((bf16[1024,2048]{1,0:T(8,128)(2,1)}), bf16[1024,8192]{1,0:T(8,128)(2,1)}) %all-gather.4.cloned.1.call-update) | async-done | bytes 16777232 | tf_op jit(solution)/shard_map/all_gather | solution.py:58
  450.4 7.5 %fusion.1 = f32[1024]{0:T(1024)S(1)} fusion(bf16[1024,8192]{1,0:T(8,128)(2,1)} %all-gather.4.cloned.1.call-done), kind=kLoop, calls=%fused_computation.4 | loop fusion | flops 25164800 | bytes 16781312 | tf_op jit(solution)/shard_map/reduce_sum | solution.py:61
  457.9 3.1 copy-done.2
  461.0 21.0 %fusion.4 = f32[1024,1024]{1,0:T(8,128)S(1)} fusion(bf16[1024,8192]{1,0:T(8,128)(2,1)S(1)} %copy-done.2, bf16[1,8192,1024]{2,1,0:T(8,128)(2,1)} %param.13, f32[8192]{0:T(1024)S(1)} %bitcast.73), kind=kOutput, calls=%fused_computation.9 | convolution fusion | flops 17205035008 | bytes 37781504 | tf_op jit(solution)/shard_map/dot_general | solution.py:60
  482.1 4.5 fusion.8
  486.6 16.3 %all-reduce.19 = (f32[1024,2]{0,1:T(2,128)}, f32[512]{0:T(512)S(1)}) all-reduce(f32[1024,2]{0,1:T(2,128)S(1)} %fusion.8, f32[512]{0:T(512)S(1)} %bitcast.66), channel_id=1, replica_groups=mesh['section'=8,'tensor'=4] {'tensor'}, use_global_device_ids=true, to_apply=%region_4.5 | all-reduce | flops 2560 | bytes 20480 | tf_op jit(solution)/shard_map/psum | solution.py:65
  502.8 3.9 all-to-all-start.1
  506.8 4.7 all-to-all-done.1
  511.6 1.0 gather_fusion
  519.4 0.7 slice.303
  522.4 0.6 slice.325
  523.1 0.6 fusion.36
  523.7 0.6 slice.310
  526.2 0.7 pad_add_fusion
  528.3 0.7 pad_maximum_fusion.1
  531.0 0.6 pad_maximum_fusion.7
  532.3 0.7 pad_maximum_fusion
  533.8 0.6 fusion.32
  534.5 12.7 %all-reduce.18 = (f32[]{:T(128)}, f32[]{:T(128)}) all-reduce(f32[]{:T(128)} %get-tuple-element.6, f32[]{:T(128)} %get-tuple-element.5), channel_id=1, replica_groups=mesh['section'=8,'tensor'=4] {'section'}, use_global_device_ids=true, to_apply=%region_10.11 | all-reduce | flops 2 | bytes 16 | tf_op jit(solution)/shard_map/psum | solution.py:73
  549.8 1.9 multiply_convert_fusion
  551.7 132.4 %all_to_all.30 = bf16[512,8,1024]{0,2,1:T(8,128)(2,1)} all-to-all(bf16[512,8,1024]{0,2,1:T(8,128)(2,1)} %bitcast.47), channel_id=1, replica_groups=mesh['section'=8,'tensor'=4] {'section'}, dimensions={1} | all-to-all | bytes 16777216 | tf_op jit(solution)/shard_map/all_to_all | solution.py:94
  684.1 11.5 %copy.29 = bf16[8,512,1024]{2,1,0:T(8,128)(2,1)} copy(bf16[8,512,1024]{1,2,0:T(8,128)(2,1)} %bitcast.48) | data formatting | bytes 16777216 | tf_op jit(solution)/shard_map/all_to_all | solution.py:94
  695.6 15.0 %fusion.44 = f32[1024,1024]{1,0:T(8,128)} fusion(bf16[4096,1024]{1,0:T(8,128)(2,1)} %bitcast.51, bf16[4096,1024]{1,0:T(8,128)(2,1)} %all-gather.8.cloned.1.call-done), kind=kOutput, calls=%fused_computation.96 | convolution fusion | flops 8589934592 | bytes 20971520 | tf_op jit(solution)/shard_map/dot_general | solution.py:96
  (145 shorter events, 13.7 us)
Async XLA Ops:
  7.2 474.9 %copy-start = (f32[1,1024,2]{1,2,0:T(2,128)S(1)}, f32[1,1024,2]{1,2,0:T(2,128)}, u32[]{:S(2)}) copy-start(f32[1,1024,2]{1,2,0:T(2,128)} %param.14) | copy-start | bytes 24580
  7.2 5.7 copy-start.3
  7.2 4.2 copy-start.5
  7.2 156.6 %all-gather.6.cloned.1.call-start = ((), (), s32[]{:S(2)}) async-start(), calls=%async_computation.4 | async-start | bytes 10485760 | tf_op jit(solution)/shard_map/all_gather | solution.py:78
  11.3 439.0 %all-gather.4.cloned.1.call-start = ((), (), s32[]{:S(2)}) async-start(), calls=%async_computation.3 | async-start | bytes 20971520 | tf_op jit(solution)/shard_map/all_gather | solution.py:58
  69.4 0.7 copy-start.8
  69.4 94.4 %copy-start.4 = (f32[8192]{0:T(1024)S(1)}, f32[8192]{0:T(1024)}, u32[]{:S(2)}) copy-start(f32[8192]{0:T(1024)} %param.15) | copy-start | bytes 98308
  169.1 15.5 %copy-start.1 = (bf16[512,8192]{0,1:T(8,128)(2,1)}, bf16[512,8192]{0,1:T(8,128)(2,1)S(1)}, u32[]{:S(2)}) copy-start(bf16[512,8192]{0,1:T(8,128)(2,1)S(1)} %get-tuple-element.14) | copy-start | bytes 25165828
  169.1 15.5 %copy-start.7 = (f32[1024]{0:T(1024)S(1)}, f32[1024]{0:T(1024)}, u32[]{:S(2)}) copy-start(f32[1024]{0:T(1024)} %param.17) | copy-start | bytes 12292
  184.6 273.3 %copy-start.9 = (f32[1,8192]{1,0:T(1,128)S(1)}, f32[1,8192]{1,0:T(1,128)}, u32[]{:S(2)}) copy-start(f32[1,8192]{1,0:T(1,128)} %param.12) | copy-start | bytes 98308
  450.4 10.7 %copy-start.2 = (bf16[1024,8192]{1,0:T(8,128)(2,1)S(1)}, bf16[1024,8192]{1,0:T(8,128)(2,1)}, u32[]{:S(2)}) copy-start(bf16[1024,8192]{1,0:T(8,128)(2,1)} %all-gather.4.cloned.1.call-done) | copy-start | bytes 50331652
  502.8 8.6 %all-to-all-start.1 = ((f32[8,128,2]{1,2,0:T(2,128)}), f32[8,128,2]{1,2,0:T(2,128)S(1)}, u32[]{:S(2)}, u32[]{:S(2)}) async-start(f32[8,128,2]{1,2,0:T(2,128)} %bitcast.12), calls=%async_computation.1 | async-start | bytes 16384 | tf_op jit(solution)/shard_map/all_to_all | solution.py:67
  506.7 188.9 %all-gather.8.cloned.1.call-start = ((), (), s32[]{:S(2)}) async-start(), calls=%async_computation.5 | async-start | bytes 9437184 | tf_op jit(solution)/shard_map/all_gather | solution.py:95
  549.8 134.4 %copy-start.6 = (f32[1,512]{1,0:T(1,128)}, f32[1,512]{1,0:T(1,128)S(1)}, u32[]{:S(2)}) copy-start(f32[1,512]{1,0:T(1,128)S(1)} %subtract_multiply_fusion.1) | copy-start | bytes 6148
Sparse Core Ops, SparseCore 0:
  11.5 152.3 all-gather.5
  165.4 284.9 all-gather.3
  551.8 119.5 all-gather.7
where the time goes:
time: 718 us; the launch traced here: 717 us
  waiting for transfers between devices  361 us (50%)
  blocking collectives  215 us (30%)
  matrix products  60.8 us (8%)
  local copies, waits for them, and re-layouts  35 us (5%)
  other arithmetic  20.5 us (3%)
  between operations  20 us (3%)
    all_gather x1, waiting for transfers between devices, body(): lax.all_gather(arrived, 'tensor', axis=1, tiled=True).astype(jnp.float32)  263 us
    all_to_all x1, blocking collectives, body(): lax.all_to_all(gained, 'section', split_axis=1, concat_axis=0, tiled=True)  132 us
    all_gather x1, waiting for transfers between devices, body(): features = lax.all_gather(states, 'tensor', axis=1, tiled=True)  93.4 us
    all_to_all x1, blocking collectives, body(): lax.all_to_all(outbox, 'section', split_axis=0, concat_axis=0, tiled=True)  54.1 us
    dot_general x1, matrix products, body(): jnp.dot(scaled, member_weight, preferred_element_type=jnp.float32)  21 us
    psum x1, blocking collectives, body(): scores = lax.psum(partial_scores, 'tensor')  16.3 us
    dot_general x1, matrix products, body(): jnp.dot(gained, actor_weight, preferred_element_type=jnp.float32)  15.5 us
    dot_general x1, matrix products, body(): lax.dot_general(blocks, every_row, (((0,), (0,)), ((), ())), preferred_el...  15 us
  transfers between devices with their start and end apart: 4, of which 3 were waited for; matrix products, arithmetic and copies ran while one was open for 5% of the time, Pallas kernels for 0%

commit v1 on v0

--- a/solution.py
+++ b/solution.py
@@ -75,7 +75,16 @@
     center = adv_total / total_tokens
     spread = adv_square / total_tokens - center * center
     advantages = (raw_adv - center) * lax.rsqrt(spread + epsilon)
-    features = lax.all_gather(states, "tensor", axis=1, tiled=True)
+    shard = states
+    ways, here, step = (lax.axis_size("tensor"), lax.axis_index("tensor"), shard.shape[1])
+    shape = [n * ways if d == 1 else n for d, n in enumerate(shard.shape)]
+    full = lax.dynamic_update_slice_in_dim(
+        jnp.zeros(shape, shard.dtype), shard, here * step, axis=1
+    )
+    for far in range(1, ways):
+        shard = lax.ppermute(shard, "tensor", [(d, (d + 1) % ways) for d in range(ways)])
+        full = lax.dynamic_update_slice_in_dim(full, shard, (here - far) % ways * step, axis=1)
+    features = full
     widened = features.astype(jnp.float32)
     actor_scale = lax.rsqrt(jnp.mean(widened * widened, axis=1) + epsilon)
     gained = (widened * actor_gain[None, :]).astype(jnp.bfloat16)

time: 718 us -> 769 us (1.071)
  starting transfers between devices: 3.98 us -> 102 us
  waiting for transfers between devices: 361 us -> 287 us
  blocking collectives: 215 us -> 236 us
    ppermute x0 -> x3, waiting for transfers between devices: none -> 254 us  [body(): lax.ppermute(shard, 'tensor', [(d, (d + 1) % ways) for d in range(ways)])]
    all_gather x1, waiting for transfers between devices: 263 us -> 28.9 us  [body(): lax.all_gather(arrived, 'tensor', axis=1, tiled=True).astype(jnp.float32)]
    ppermute x0 -> x3, starting transfers between devices: none -> 98.4 us  [body(): lax.ppermute(shard, 'tensor', [(d, (d + 1) % ways) for d in range(ways)])]
    all_gather x1 -> x0, waiting for transfers between devices: 93.4 us -> none  [body(): features = lax.all_gather(states, 'tensor', axis=1, tiled=True)]
    psum x1, blocking collectives: 16.3 us -> 37.1 us  [body(): scores = lax.psum(partial_scores, 'tensor')]
  transfers between devices with their start and end apart: 4 -> 6, of which waited for: 3 -> 5; matrix products, arithmetic and copies ran while one was open for 5% -> 5% of each run, Pallas kernels for 0% -> 0%
where the time goes in v1:
time: 769 us; the launch traced here: 768 us
  waiting for transfers between devices  287 us (37%)
  blocking collectives  236 us (31%)
  starting transfers between devices  102 us (13%)
  matrix products  61.8 us (8%)
  local copies, waits for them, and re-layouts  40.5 us (5%)
  between operations  20.3 us (3%)
  other arithmetic  19.9 us (3%)
    ppermute x3, waiting for transfers between devices, body(): lax.ppermute(shard, 'tensor', [(d, (d + 1) % ways) for d in range(ways)])  254 us
    all_to_all x1, blocking collectives, body(): lax.all_to_all(gained, 'section', split_axis=1, concat_axis=0, tiled=True)  132 us
    ppermute x3, starting transfers between devices, body(): lax.ppermute(shard, 'tensor', [(d, (d + 1) % ways) for d in range(ways)])  98.4 us
    all_to_all x1, blocking collectives, body(): lax.all_to_all(outbox, 'section', split_axis=0, concat_axis=0, tiled=True)  54.1 us
    psum x1, blocking collectives, body(): scores = lax.psum(partial_scores, 'tensor')  37.1 us
    all_gather x1, waiting for transfers between devices, body(): lax.all_gather(arrived, 'tensor', axis=1, tiled=True).astype(jnp.float32)  28.9 us
    dot_general x1, matrix products, body(): jnp.dot(scaled, member_weight, preferred_element_type=jnp.float32)  21 us
  transfers between devices with their start and end apart: 6, of which 5 were waited for; matrix products, arithmetic and copies ran while one was open for 5% of the time, Pallas kernels for 0%

profile of v1, /device:TPU:0, one launch (start us, length us, event | category | flops | bytes accessed | tf_op | source)
XLA Modules:
  0.0 768.0 jit_solution(395803632757429264)
XLA Ops:
  7.9 1.1 reduce-window.14
  9.3 0.8 fusion.25
  10.8 3.9 convolution_convert_fusion
  14.7 54.1 %all_to_all.29 = bf16[8,128,2048]{2,1,0:T(8,128)(2,1)} all-to-all(bf16[8,128,2048]{2,1,0:T(8,128)(2,1)S(1)} %bitcast.52), channel_id=1, replica_groups=mesh['section'=8,'tensor'=4] {'section'}, dimensions={0} | all-to-all | bytes 8388608 | tf_op jit(solution)/shard_map/all_to_all | solution.py:52
  68.9 2.9 copy.30
  71.7 1.6 collective-permute-start
  73.4 84.6 %collective-permute-done = bf16[512,2048]{0,1:T(8,128)(2,1)S(1)} collective-permute-done((bf16[512,2048]{0,1:T(8,128)(2,1)S(1)}, bf16[512,2048]{0,1:T(8,128)(2,1)S(1)}, u32[]{:S(2)}, u32[]{:S(2)}) %collective-permute-start) | collective-permute-done | bytes 2097184 | tf_op jit(solution)/shard_map/ppermute | solution.py:85
  157.9 1.3 copy-done.3
  159.2 43.0 %collective-permute-start.1 = (bf16[512,2048]{0,1:T(8,128)(2,1)S(1)}, bf16[512,2048]{0,1:T(8,128)(2,1)}, u32[]{:S(2)}, u32[]{:S(2)}) collective-permute-start(bf16[512,2048]{0,1:T(8,128)(2,1)S(1)} %collective-permute-done), channel_id=1, source_target_pairs={{0,1},{1,2},{2,3},{3,0},{4,5},{5,6},{6,7},{7,4},{8,9},{9,10},{10,1... | collective-permute-start | bytes 6291464 | tf_op jit(solution)/shard_map/ppermute | solution.py:85
  202.3 85.7 %collective-permute-done.1 = bf16[512,2048]{0,1:T(8,128)(2,1)} collective-permute-done((bf16[512,2048]{0,1:T(8,128)(2,1)S(1)}, bf16[512,2048]{0,1:T(8,128)(2,1)}, u32[]{:S(2)}, u32[]{:S(2)}) %collective-permute-start.1) | collective-permute-done | bytes 2097184 | tf_op jit(solution)/shard_map/ppermute | solution.py:85
  288.0 53.7 %collective-permute-start.2 = (bf16[512,2048]{0,1:T(8,128)(2,1)}, bf16[512,2048]{0,1:T(8,128)(2,1)}, u32[]{:S(2)}, u32[]{:S(2)}) collective-permute-start(bf16[512,2048]{0,1:T(8,128)(2,1)} %collective-permute-done.1), channel_id=1, source_target_pairs={{0,1},{1,2},{2,3},{3,0},{4,5},{5,6},{6,7},{7,4},{8,9},{9,10},{10,1... | collective-permute-start | bytes 6291464 | tf_op jit(solution)/shard_map/ppermute | solution.py:85
  342.9 1.3 copy-done.4
  344.5 1.8 constant_dynamic-update-slice_fusion.1
  346.3 83.7 %collective-permute-done.2 = bf16[512,2048]{0,1:T(8,128)(2,1)} collective-permute-done((bf16[512,2048]{0,1:T(8,128)(2,1)}, bf16[512,2048]{0,1:T(8,128)(2,1)}, u32[]{:S(2)}, u32[]{:S(2)}) %collective-permute-start.2) | collective-permute-done | bytes 2097184 | tf_op jit(solution)/shard_map/ppermute | solution.py:85
  429.9 1.8 constant_dynamic-update-slice_fusion
  431.8 2.6 fusion.3
  434.4 14.9 %fusion.43 = f32[512,1024]{1,0:T(8,128)S(1)} fusion(bf16[512,8192]{0,1:T(8,128)(2,1)S(1)} %get-tuple-element.14, bf16[8192,1024]{1,0:T(8,128)(2,1)} %param.16), kind=kOutput, calls=%fused_computation.99 | convolution fusion | flops 8589934592 | bytes 27262976 | tf_op jit(solution)/shard_map/dot_general | solution.py:92
  449.3 2.4 fusion.15
  451.7 28.9 %all-gather.3.cloned.1.call-done = bf16[1024,8192]{1,0:T(8,128)(2,1)} async-done(((bf16[1024,2048]{1,0:T(8,128)(2,1)}), bf16[1024,8192]{1,0:T(8,128)(2,1)}) %all-gather.3.cloned.1.call-update) | async-done | bytes 16777232 | tf_op jit(solution)/shard_map/all_gather | solution.py:58
  480.6 7.5 fusion.1
  488.1 3.1 copy-done.2
  491.3 21.0 %fusion.4 = f32[1024,1024]{1,0:T(8,128)S(1)} fusion(bf16[1024,8192]{1,0:T(8,128)(2,1)S(1)} %copy-done.2, bf16[1,8192,1024]{2,1,0:T(8,128)(2,1)} %param.13, f32[8192]{0:T(1024)S(1)} %bitcast.73), kind=kOutput, calls=%fused_computation.9 | convolution fusion | flops 17205035008 | bytes 37781504 | tf_op jit(solution)/shard_map/dot_general | solution.py:60
  512.3 4.5 fusion.8
  516.8 37.1 %all-reduce.19 = (f32[1024,2]{0,1:T(2,128)}, f32[512]{0:T(512)S(1)}) all-reduce(f32[1024,2]{0,1:T(2,128)S(1)} %fusion.8, f32[512]{0:T(512)S(1)} %bitcast.66), channel_id=1, replica_groups=mesh['section'=8,'tensor'=4] {'tensor'}, use_global_device_ids=true, to_apply=%region_4.5 | all-reduce | flops 2560 | bytes 20480 | tf_op jit(solution)/shard_map/psum | solution.py:65
  554.0 3.3 all-to-all-start.1
  557.4 4.6 all-to-all-done.1
  562.2 1.0 gather_fusion
  585.0 12.6 %all-reduce.18 = (f32[]{:T(128)}, f32[]{:T(128)}) all-reduce(f32[]{:T(128)} %get-tuple-element.6, f32[]{:T(128)} %get-tuple-element.5), channel_id=1, replica_groups=mesh['section'=8,'tensor'=4] {'section'}, use_global_device_ids=true, to_apply=%region_10.11 | all-reduce | flops 2 | bytes 16 | tf_op jit(solution)/shard_map/psum | solution.py:73
  600.3 1.9 multiply_convert_fusion
  602.2 132.5 %all_to_all.30 = bf16[512,8,1024]{0,2,1:T(8,128)(2,1)} all-to-all(bf16[512,8,1024]{0,2,1:T(8,128)(2,1)} %bitcast.47), channel_id=1, replica_groups=mesh['section'=8,'tensor'=4] {'section'}, dimensions={1} | all-to-all | bytes 16777216 | tf_op jit(solution)/shard_map/all_to_all | solution.py:103
  734.7 11.5 %copy.32 = bf16[8,512,1024]{2,1,0:T(8,128)(2,1)} copy(bf16[8,512,1024]{1,2,0:T(8,128)(2,1)} %bitcast.48) | data formatting | bytes 16777216 | tf_op jit(solution)/shard_map/all_to_all | solution.py:103
  746.2 15.0 %fusion.44 = f32[1024,1024]{1,0:T(8,128)} fusion(bf16[4096,1024]{1,0:T(8,128)(2,1)} %bitcast.51, bf16[4096,1024]{1,0:T(8,128)(2,1)} %all-gather.5.cloned.1.call-done), kind=kOutput, calls=%fused_computation.100 | convolution fusion | flops 8589934592 | bytes 20971520 | tf_op jit(solution)/shard_map/dot_general | solution.py:105
  (155 shorter events, 21.8 us)
Async XLA Ops:
  7.2 505.1 %copy-start = (f32[1,1024,2]{1,2,0:T(2,128)S(1)}, f32[1,1024,2]{1,2,0:T(2,128)}, u32[]{:S(2)}) copy-start(f32[1,1024,2]{1,2,0:T(2,128)} %param.14) | copy-start | bytes 24580
  7.2 473.4 %all-gather.3.cloned.1.call-start = ((), (), s32[]{:S(2)}) async-start(), calls=%async_computation.3 | async-start | bytes 20971520 | tf_op jit(solution)/shard_map/all_gather | solution.py:58
  68.8 272.8 %copy-start.9 = (s32[1,16]{1,0:T(1,128)S(1)}, s32[1,16]{1,0:T(1,128)}, u32[]{:S(2)}) copy-start(s32[1,16]{1,0:T(1,128)} %param.10) | copy-start | bytes 196
  68.8 273.2 %copy-start.6 = (s32[512,1]{0,1:T(1,128)S(1)}, s32[512,1]{0,1:T(1,128)}, u32[]{:S(2)}) copy-start(s32[512,1]{0,1:T(1,128)} %param.11) | copy-start | bytes 6148
  71.7 86.2 %collective-permute-start = (bf16[512,2048]{0,1:T(8,128)(2,1)S(1)}, bf16[512,2048]{0,1:T(8,128)(2,1)S(1)}, u32[]{:S(2)}, u32[]{:S(2)}) collective-permute-start(bf16[512,2048]{0,1:T(8,128)(2,1)S(1)} %copy.30), channel_id=1, source_target_pairs={{0,1},{1,2},{2,3},{3,0},{4,5},{5,6},{6,7},{7,4},{8,9},{9,10},{10,1... | collective-permute-start | bytes 6291464 | tf_op jit(solution)/shard_map/ppermute | solution.py:85
  157.9 1.3 copy-start.3
  159.2 128.7 %collective-permute-start.1 = (bf16[512,2048]{0,1:T(8,128)(2,1)S(1)}, bf16[512,2048]{0,1:T(8,128)(2,1)}, u32[]{:S(2)}, u32[]{:S(2)}) collective-permute-start(bf16[512,2048]{0,1:T(8,128)(2,1)S(1)} %collective-permute-done), channel_id=1, source_target_pairs={{0,1},{1,2},{2,3},{3,0},{4,5},{5,6},{6,7},{7,4},{8,9},{9,10},{10,1... | collective-permute-start | bytes 6291464 | tf_op jit(solution)/shard_map/ppermute | solution.py:85
  288.0 142.0 %collective-permute-start.2 = (bf16[512,2048]{0,1:T(8,128)(2,1)}, bf16[512,2048]{0,1:T(8,128)(2,1)}, u32[]{:S(2)}, u32[]{:S(2)}) collective-permute-start(bf16[512,2048]{0,1:T(8,128)(2,1)} %collective-permute-done.1), channel_id=1, source_target_pairs={{0,1},{1,2},{2,3},{3,0},{4,5},{5,6},{6,7},{7,4},{8,9},{9,10},{10,1... | collective-permute-start | bytes 6291464 | tf_op jit(solution)/shard_map/ppermute | solution.py:85
  342.6 1.6 copy-start.4
  344.4 87.3 %copy-start.5 = (f32[8192]{0:T(1024)S(1)}, f32[8192]{0:T(1024)}, u32[]{:S(2)}) copy-start(f32[8192]{0:T(1024)} %param.15) | copy-start | bytes 98308
  434.3 15.0 %copy-start.1 = (bf16[512,8192]{0,1:T(8,128)(2,1)}, bf16[512,8192]{0,1:T(8,128)(2,1)S(1)}, u32[]{:S(2)}) copy-start(bf16[512,8192]{0,1:T(8,128)(2,1)S(1)} %get-tuple-element.14) | copy-start | bytes 25165828
  434.3 14.9 %copy-start.8 = (f32[1024]{0:T(1024)S(1)}, f32[1024]{0:T(1024)}, u32[]{:S(2)}) copy-start(f32[1024]{0:T(1024)} %param.17) | copy-start | bytes 12292
  449.3 38.8 %copy-start.10 = (f32[1,8192]{1,0:T(1,128)S(1)}, f32[1,8192]{1,0:T(1,128)}, u32[]{:S(2)}) copy-start(f32[1,8192]{1,0:T(1,128)} %param.12) | copy-start | bytes 98308
  480.6 10.7 %copy-start.2 = (bf16[1024,8192]{1,0:T(8,128)(2,1)S(1)}, bf16[1024,8192]{1,0:T(8,128)(2,1)}, u32[]{:S(2)}) copy-start(bf16[1024,8192]{1,0:T(8,128)(2,1)} %all-gather.3.cloned.1.call-done) | copy-start | bytes 50331652
  554.0 8.0 %all-to-all-start.1 = ((f32[8,128,2]{1,2,0:T(2,128)}), f32[8,128,2]{1,2,0:T(2,128)S(1)}, u32[]{:S(2)}, u32[]{:S(2)}) async-start(f32[8,128,2]{1,2,0:T(2,128)} %bitcast.12), calls=%async_computation.1 | async-start | bytes 16384 | tf_op jit(solution)/shard_map/all_to_all | solution.py:67
  557.3 188.9 %all-gather.5.cloned.1.call-start = ((), (), s32[]{:S(2)}) async-start(), calls=%async_computation.4 | async-start | bytes 9437184 | tf_op jit(solution)/shard_map/all_gather | solution.py:104
  600.3 134.4 %copy-start.7 = (f32[1,512]{1,0:T(1,128)}, f32[1,512]{1,0:T(1,128)S(1)}, u32[]{:S(2)}) copy-start(f32[1,512]{1,0:T(1,128)S(1)} %subtract_multiply_fusion.1) | copy-start | bytes 6148
Sparse Core Ops, SparseCore 0:
  69.0 411.5 all-gather.2
  602.3 119.0 all-gather.4
